TPU v7x, 32 devices: a whole 2x2x4 slice. The times are simulated.
32 devices in a mesh: expert: 16 (over z, y, core), dp: 2 (over x).
Axes of the slice: x: 2, y: 2, z: 4, core: 2. Of those that a mesh axis runs over, the one named last changes fastest.
Arguments:
- tokens: bfloat16 [4096, 2048], P(('expert', 'dp')), may hold values from -6 to 6
- cotangent: bfloat16 [4096, 2048], P(('expert', 'dp')), may hold values from -6 to 6
- routes: int32 [4096, 8], P(('expert', 'dp')), may hold values from 0 to 15, all different within a row; in each aligned block of 128 rows (0 to 127, 128 to 255, ...) at most 72 rows name the same one
- route_weight: float32 [4096, 8], P(('expert', 'dp')), may hold values from 0.05 to 1
- gate_weight: bfloat16 [16, 768, 2048], P('expert', 'dp'), may hold values from -6 to 6
- up_weight: bfloat16 [16, 768, 2048], P('expert', 'dp'), may hold values from -6 to 6
- down_weight: bfloat16 [16, 768, 2048], P('expert', 'dp'), may hold values from -6 to 6
- cluster_of: int32 [16], replicated, may hold values from 0 to 7, as said below
- owner: int32 [8], replicated, may hold values from 0 to 7, each once
Outputs:
- merged_gate: bfloat16 [16, 768, 1024], P('expert', 'dp')
- merged_up: bfloat16 [16, 768, 1024], P('expert', 'dp')
- merged_down: bfloat16 [16, 768, 1024], P('expert', 'dp')
- share: float32 [16, 768], P('expert', 'dp')
Inputs may be any that keep to these rules, and one draw needn't show every extreme that they name: `routes`: at most 72 of the rows of one device name the same expert, and every expert is named by at least one row. `cluster_of`: every one of the 8 clusters has at least one member. Each owner pair owns exactly one cluster.
All inputs are finite; a program needn't handle non-finite values.
Results may differ from a plain program's by a relative error of at most 0.0014.
Values may be sent and summed in bfloat16 or wider, within the bound.
A program may use at most 128 MiB of HBM per device.

v0:
```python
import functools

import jax
import jax.numpy as jnp
from jax import lax
from jax.experimental import pallas as pl
from jax.experimental.pallas import tpu as pltpu
from jax.sharding import PartitionSpec as P

LANES = 128
MESH = pl.DeviceIdType.MESH


def spread_kernel(
    tokens_ref, gate_ref, up_ref, down_ref, got_ref, fisher_ref,
    rows_ref, held_ref, parts_ref, others_ref, block_ref,
    token_send, token_recv, piece_send, piece_recv, swap_send, swap_recv,
    part_send, part_recv, share_send, share_recv, local_sem,
    *, factor,
):
    experts, dp_count = lax.axis_size("expert"), lax.axis_size("dp")
    depth = experts // 4
    me, my_dp = lax.axis_index("expert"), lax.axis_index("dp")
    z, y, core = me // 4, (me // 2) % 2, me % 2
    row_count = tokens_ref.shape[0]
    model_width = gate_ref.shape[1]
    half_cols = model_width // 2
    piece_rows = got_ref.shape[2]
    weights = (gate_ref, up_ref, down_ref)
    far_side, near_side = (1 - z // (depth // 2)) * (depth // 2), z // (depth // 2) * (depth // 2)
    peers = [
        (far_side + (z + dz) % (depth // 2)) * 4 + (me + k) % 4 for k in (0, 2, 1, 3) for dz in range(depth // 2)
    ] + [
        (near_side + (z + dz) % (depth // 2)) * 4 + (me + k) % 4 for dz in range(1, depth // 2) for k in (0, 2, 1, 3)
    ] + [z * 4 + (me + k) % 4 for k in (2, 1, 3)]
    dp_of = [(my_dp + k) % dp_count for k in range(dp_count)]

    barrier = pltpu.get_barrier_semaphore()
    for peer in peers:
        pl.semaphore_signal(barrier, inc=1, device_id={"expert": peer}, device_id_type=MESH)
    for other in dp_of[1:]:
        pl.semaphore_signal(barrier, inc=1, device_id={"dp": other}, device_id_type=MESH)
    own = [
        pltpu.make_async_copy(tokens_ref, rows_ref.at[me], local_sem.at[0]),
        pltpu.make_async_copy(gate_ref, held_ref.at[0, 0], local_sem.at[1]),
        pltpu.make_async_copy(up_ref, held_ref.at[0, 1], local_sem.at[2]),
        pltpu.make_async_copy(
            down_ref.at[pl.ds((me // 2) * piece_rows, piece_rows), pl.ds((me % 2) * half_cols, half_cols)],
            block_ref, local_sem.at[3],
        ),
    ]
    for copy in own:
        copy.start()
    pl.semaphore_wait(barrier, experts - 1 + dp_count - 1)

    def token_copy(slot, kind, peer, source=None):
        return pltpu.make_async_remote_copy(
            src_ref=rows_ref.at[slot] if source is None else source,
            dst_ref=rows_ref.at[slot],
            send_sem=token_send.at[kind, slot],
            recv_sem=token_recv.at[slot],
            device_id={"expert": peer},
            device_id_type=MESH,
        )

    across = z * 4 + (1 - y) * 2 + core
    partner = z * 4 + y * 2 + (1 - core)

    def line(act):
        source = tokens_ref
        for sign, kind in ((1, 0), (-1, 1)):
            @pl.when((z + sign >= 0) & (z + sign < depth))
            def _():
                act(token_copy(me, kind, me + 4 * sign, source), None)
        act(token_copy(me, 2, across, source), None)
        act(token_copy(me, 3, partner, source), None)
        for distance in range(1, depth):
            for sign, kind in ((1, 0), (-1, 1)):
                origin = z - sign * distance

                @pl.when((origin >= 0) & (origin < depth))
                def _():
                    slot = origin * 4 + y * 2 + core
                    act(None, slot)

                    @pl.when((z + sign >= 0) & (z + sign < depth))
                    def _():
                        act(token_copy(slot, kind, me + 4 * sign), None)
                    act(token_copy(slot, 2, across), None)
                    act(token_copy(slot, 3, partner), None)

    def beside(act):
        for distance in range(depth):
            for sign in (1, -1) if distance else (1,):
                origin = z - sign * distance

                @pl.when((origin >= 0) & (origin < depth))
                def _():
                    slot = origin * 4 + (1 - y) * 2 + core
                    act(None, slot)
                    act(token_copy(slot, 3, partner), None)

    def begin(copy, slot):
        if copy is None:
            token_copy(slot, 0, partner).wait_recv()
        else:
            copy.start()

    def finish(copy, slot):
        if copy is not None:
            copy.wait_send()

    def piece_copy(which, peer, landing):
        return pltpu.make_async_remote_copy(
            src_ref=weights[which].at[
                pl.ds((peer // 2) * piece_rows, piece_rows), pl.ds((peer % 2) * half_cols, half_cols)
            ],
            dst_ref=got_ref.at[landing, which],
            send_sem=piece_send.at[peer, which],
            recv_sem=piece_recv.at[landing, which],
            device_id={"expert": peer},
            device_id_type=MESH,
        )

    def swap_copy(shift, which):
        return pltpu.make_async_remote_copy(
            src_ref=weights[which],
            dst_ref=held_ref.at[shift, which],
            send_sem=swap_send.at[shift, which],
            recv_sem=swap_recv.at[shift, which],
            device_id={"dp": dp_of[(dp_count - shift) % dp_count]},
            device_id_type=MESH,
        )

    swaps = [swap_copy(shift, which) for shift in range(1, dp_count) for which in range(2)]
    for copy in swaps:
        copy.start()
    line(begin)
    for peer in peers:
        for which in range(3):
            piece_copy(which, peer, me).start()
    for copy in own:
        copy.wait()
    keep = [
        pltpu.make_async_copy(
            held_ref.at[0, which, pl.ds((me // 2) * piece_rows, piece_rows), pl.ds((me % 2) * half_cols, half_cols)],
            got_ref.at[me, which], local_sem.at[which],
        )
        for which in range(2)
    ] + [pltpu.make_async_copy(block_ref, got_ref.at[me, 2], local_sem.at[2])]
    for copy in keep:
        copy.start()
    beside(begin)
    for zs in range(depth):
        for ys in range(2):
            token_copy(zs * 4 + ys * 2 + 1 - core, 0, partner).wait_recv()

    contract = (((1,), (1,)), ((), ()))
    group = 4 if experts % 4 == 0 else 1
    for shift in range(dp_count):
        if shift:
            for which in range(2):
                swap_copy(shift, which).wait_recv()
        parts_ref[shift] = jnp.zeros_like(parts_ref[shift])

        def step(index, carry):
            block = rows_ref[pl.ds(index * group, group)].reshape(group * row_count, rows_ref.shape[2])
            tokens = block[:, :model_width]
            pre_gate = lax.dot_general(
                tokens, held_ref[shift, 0], contract, preferred_element_type=jnp.float32) * factor
            pre_up = lax.dot_general(
                tokens, held_ref[shift, 1], contract, preferred_element_type=jnp.float32) * factor
            act = pre_gate / (1.0 + jnp.exp(-pre_gate)) * pre_up
            columns = block[:, model_width:].astype(jnp.float32)
            lane = lax.broadcasted_iota(jnp.int32, columns.shape, 1)
            scale = jnp.sum(jnp.where(lane == me, columns, 0.0), axis=1, keepdims=True)
            parts_ref[shift] += jnp.sum(act * act * scale, axis=0, keepdims=True)
            return carry

        lax.fori_loop(0, experts // group, step, 0)

    def part_copy(shift):
        return pltpu.make_async_remote_copy(
            src_ref=parts_ref.at[shift],
            dst_ref=others_ref.at[shift],
            send_sem=part_send.at[shift],
            recv_sem=part_recv.at[shift],
            device_id={"dp": dp_of[shift]},
            device_id_type=MESH,
        )

    for shift in range(1, dp_count):
        part_copy(shift).start()
    total = parts_ref[0]
    for shift in range(1, dp_count):
        part_copy(shift).wait()
        total = total + others_ref[shift]
    fisher_ref[me] = total

    def share_copy(peer, landing):
        return pltpu.make_async_remote_copy(
            src_ref=fisher_ref.at[me],
            dst_ref=fisher_ref.at[landing],
            send_sem=share_send.at[peer],
            recv_sem=share_recv.at[landing],
            device_id={"expert": peer},
            device_id_type=MESH,
        )

    for peer in peers:
        share_copy(peer, me).start()
    line(finish)
    beside(finish)
    for copy in swaps:
        copy.wait_send()
    for copy in keep:
        copy.wait()
    for peer in peers:
        share_copy(peer, me).wait_send()
        pltpu.make_async_remote_copy(
            src_ref=fisher_ref.at[me], dst_ref=fisher_ref.at[peer], send_sem=share_send.at[peer],
            recv_sem=share_recv.at[peer], device_id={"expert": peer}, device_id_type=MESH,
        ).wait_recv()
        for which in range(3):
            piece_copy(which, peer, me).wait_send()
            piece_copy(which, peer, peer).wait_recv()


def spread(extended, gate, up, down):
    experts, dp_count = lax.axis_size("expert"), lax.axis_size("dp")
    row_count, wide = extended.shape
    hid_dev, model_width = gate.shape
    piece_rows, half_cols = hid_dev // (experts // 2), model_width // 2
    anywhere = pl.BlockSpec(memory_space=pl.ANY)
    dma = pltpu.SemaphoreType.DMA
    got, fisher = pl.pallas_call(
        functools.partial(spread_kernel, factor=1.0 / float(model_width) ** 0.5),
        out_shape=(
            jax.ShapeDtypeStruct((experts, 3, piece_rows, half_cols), jnp.bfloat16),
            jax.ShapeDtypeStruct((experts, 1, hid_dev), jnp.float32),
        ),
        in_specs=[anywhere] * 4,
        out_specs=(anywhere, pl.BlockSpec(memory_space=pltpu.VMEM)),
        scratch_shapes=[
            pltpu.VMEM((experts, row_count, wide), jnp.bfloat16),
            pltpu.VMEM((dp_count, 2, hid_dev, model_width), jnp.bfloat16),
            pltpu.VMEM((dp_count, 1, hid_dev), jnp.float32),
            pltpu.VMEM((dp_count, 1, hid_dev), jnp.float32),
            pltpu.VMEM((piece_rows, half_cols), jnp.bfloat16),
            dma((4, experts)), dma((experts,)),
            dma((experts, 3)), dma((experts, 3)),
            dma((dp_count, 2)), dma((dp_count, 2)),
            dma((dp_count,)), dma((dp_count,)),
            dma((experts,)), dma((experts,)),
            dma((4,)),
        ],
        compiler_params=pltpu.CompilerParams(
            collective_id=0, has_side_effects=True, vmem_limit_bytes=60 * 1024 * 1024
        ),
        name="spread",
    )(extended, gate, up, down)
    return got.reshape(experts, 3 * piece_rows, half_cols), fisher[:, 0, :]


def merge_kernel(place_ref, share_ref, got_ref, out_ref, total_ref):
    total_ref[...] = jnp.zeros_like(total_ref)

    def add(expert, carry):
        place = place_ref[expert]
        weighted = got_ref[expert].astype(jnp.float32) * share_ref[expert]
        total_ref[place] = total_ref[place] + weighted
        return carry

    lax.fori_loop(0, got_ref.shape[0], add, 0)
    out_ref[...] = total_ref[...].astype(jnp.bfloat16)


def merge_blocks(place, share, got, clusters):
    shape = (clusters,) + got.shape[1:]
    return pl.pallas_call(
        merge_kernel,
        out_shape=jax.ShapeDtypeStruct(shape, jnp.bfloat16),
        in_specs=[
            pl.BlockSpec(memory_space=pltpu.SMEM),
            pl.BlockSpec(memory_space=pltpu.VMEM),
            pl.BlockSpec(memory_space=pltpu.VMEM),
        ],
        out_specs=pl.BlockSpec(memory_space=pltpu.VMEM),
        scratch_shapes=[pltpu.VMEM(shape, jnp.float32)],
        cost_estimate=pl.CostEstimate(flops=2 * got.size, bytes_accessed=3 * got.size, transcendentals=0),
        name="merge",
    )(place, share, got)


def routed_fisher(tokens, scales, routes, gate_weight, up_weight, capacity):
    expert_count = lax.axis_size("expert")
    row_count, model_width = tokens.shape
    top_count = routes.shape[1]
    scales = scales.reshape(-1)
    flat_ids = routes.reshape(-1)
    one_hot = (flat_ids[:, None] == jnp.arange(expert_count, dtype=jnp.int32)[None, :]).astype(
        jnp.int32
    )
    rank_ids = jnp.sum((jnp.cumsum(one_hot, axis=0) - one_hot) * one_hot, axis=1)
    slot_ids = flat_ids * capacity + rank_ids
    source = jnp.arange(row_count * top_count, dtype=jnp.int32) // top_count
    send_rows = (
        jnp.zeros((expert_count * capacity, model_width), jnp.bfloat16)
        .at[slot_ids]
        .set(tokens[source])
    )
    send_scales = jnp.zeros((expert_count * capacity,), jnp.bfloat16).at[slot_ids].set(scales)
    recv_rows, recv_scales = (
        lax.all_to_all(
            send_rows.reshape(expert_count, capacity, model_width),
            "expert",
            split_axis=0,
            concat_axis=0,
            tiled=True,
        ),
        lax.all_to_all(
            send_scales.reshape(expert_count, capacity),
            "expert",
            split_axis=0,
            concat_axis=0,
            tiled=True,
        ),
    )
    inputs = recv_rows.reshape(-1, model_width)
    weights_s = recv_scales.reshape(-1).astype(jnp.float32)
    hid_dev = gate_weight.shape[1]
    factor = 1.0 / jnp.sqrt(jnp.float32(model_width))
    pre_gate = (
        jnp.dot(
            inputs,
            lax.all_gather(gate_weight[0], "dp", axis=0, tiled=True).T,
            preferred_element_type=jnp.float32,
        )
        * factor
    )
    pre_up = (
        jnp.dot(
            inputs,
            lax.all_gather(up_weight[0], "dp", axis=0, tiled=True).T,
            preferred_element_type=jnp.float32,
        )
        * factor
    )
    act = jax.nn.silu(pre_gate) * pre_up
    part = jnp.dot(weights_s, act * act, precision=lax.Precision.HIGHEST)
    whole_sum = lax.psum(part, "dp")
    own_fisher = lax.dynamic_slice_in_dim(whole_sum, lax.axis_index("dp") * hid_dev, hid_dev)
    return lax.all_gather(own_fisher[None, :], "expert", axis=0, tiled=True)


def deliver_kernel(
    place_ref, share_ref, got_ref, gate_ref, up_ref, down_ref, merged_ref, send_sem, recv_sem, local_sem,
):
    experts = lax.axis_size("expert")
    chips = experts // 2
    me = lax.axis_index("expert")
    chip, core = me // 2, me % 2
    outs = (gate_ref, up_ref, down_ref)
    piece_rows = gate_ref.shape[1]
    places = [(chip + k) % chips for k in sorted(range(1, chips), key=lambda k: abs(k - chips // 2))] + [chip]

    barrier = pltpu.get_barrier_semaphore()
    for place in places[:-1]:
        pl.semaphore_signal(barrier, inc=1, device_id={"expert": 2 * place + core}, device_id_type=MESH)
    pl.semaphore_wait(barrier, chips - 1)

    def remote(place, which, landing):
        return pltpu.make_async_remote_copy(
            src_ref=merged_ref.at[place, pl.ds(which * piece_rows, piece_rows)],
            dst_ref=outs[which].at[landing],
            send_sem=send_sem.at[place, which],
            recv_sem=recv_sem.at[landing, which],
            device_id={"expert": 2 * place + core},
            device_id_type=MESH,
        )

    tall = 16
    for place in places:
        for which in range(3):
            def rows(index, carry):
                at = pl.ds(pl.multiple_of(which * piece_rows + index * tall, tall), tall)
                total = jnp.zeros((tall, got_ref.shape[2]), jnp.float32)
                for expert in range(experts):
                    part = jnp.where(place_ref[expert] == place, share_ref[expert, at], 0.0)
                    total = total + got_ref[expert, at].astype(jnp.float32) * part
                merged_ref[place, at] = total.astype(jnp.bfloat16)
                return carry

            lax.fori_loop(0, piece_rows // tall, rows, 0)
            if place is not places[-1]:
                remote(place, which, chip).start()
    keep = [
        pltpu.make_async_copy(
            merged_ref.at[chip, pl.ds(which * piece_rows, piece_rows)], outs[which].at[chip], local_sem.at[which]
        )
        for which in range(3)
    ]
    for copy in keep:
        copy.start()
    for copy in keep:
        copy.wait()
    for place in places[:-1]:
        for which in range(3):
            remote(place, which, chip).wait_send()
            remote(place, which, place).wait_recv()


def deliver(place, share, got):
    experts, rows, half_cols = got.shape
    chips = experts // 2
    vmem = pl.BlockSpec(memory_space=pltpu.VMEM)
    dma = pltpu.SemaphoreType.DMA
    return pl.pallas_call(
        deliver_kernel,
        out_shape=tuple(jax.ShapeDtypeStruct((chips, rows // 3, half_cols), jnp.bfloat16) for _ in range(3)),
        in_specs=[pl.BlockSpec(memory_space=pltpu.SMEM), vmem, vmem],
        out_specs=(pl.BlockSpec(memory_space=pl.ANY),) * 3,
        scratch_shapes=[
            pltpu.VMEM((chips, rows, half_cols), jnp.bfloat16),
            dma((chips, 3)), dma((chips, 3)), dma((3,)),
        ],
        compiler_params=pltpu.CompilerParams(
            collective_id=1, has_side_effects=True, vmem_limit_bytes=40 * 1024 * 1024
        ),
        name="deliver",
    )(place, share, got)


def with_scales(tokens, scales, routes):
    scale_cols = -(-lax.axis_size("expert") // LANES) * LANES
    chosen = routes[:, :, None] == jnp.arange(scale_cols, dtype=jnp.int32)[None, None, :]
    scale_of = jnp.sum(jnp.where(chosen, scales[:, :, None].astype(jnp.float32), 0.0), axis=1)
    return jnp.concatenate([tokens, scale_of.astype(jnp.bfloat16)], axis=1)


def exchange(*weights):
    expert_count = lax.axis_size("expert")
    blocks, (_, hid_dev, model_width) = expert_count // 2, weights[0].shape

    def split(weight):
        return weight[0].reshape(blocks, hid_dev // blocks, 2, model_width // 2).transpose(0, 2, 1, 3)

    sent = jnp.stack([split(w) for w in weights], axis=2)
    sent = sent.reshape(expert_count, 3 * (hid_dev // blocks), model_width // 2)
    return lax.all_to_all(sent, "expert", split_axis=0, concat_axis=0, tiled=True)


def per_device(
    tokens, cotangent, routes, route_weight, gate_weight, up_weight, down_weight, cluster_of, owner
):
    expert_count = lax.axis_size("expert")
    row_count, model_width = tokens.shape
    top_count = routes.shape[1]
    capacity = max(2, row_count * top_count * 9 // (8 * expert_count))
    energy = jnp.mean(jnp.square(cotangent.astype(jnp.float32)), axis=1)
    scales = (jnp.square(route_weight) * energy[:, None]).astype(jnp.bfloat16)
    hid_dev = gate_weight.shape[1]
    half_cols = model_width // 2
    blocks = expert_count // 2
    block_rows = hid_dev // blocks

    dense = row_count <= 2 * capacity and expert_count % 8 == 0 and block_rows % 16 == 0
    if dense:
        extended = with_scales(tokens, scales, routes)
        got, peer_fisher = spread(extended, gate_weight[0], up_weight[0], down_weight[0])
    else:
        got = exchange(gate_weight, up_weight, down_weight)
        peer_fisher = routed_fisher(tokens, scales, routes, gate_weight, up_weight, capacity)
    clusters = owner.shape[0]
    same = (cluster_of[None, :] == cluster_of[:, None]).astype(jnp.float32)
    share_all = peer_fisher / jnp.dot(same, peer_fisher, precision=lax.Precision.HIGHEST)
    my_index = lax.axis_index("expert")
    share = lax.dynamic_slice_in_dim(share_all, my_index, 1, 0)
    window = lax.dynamic_slice_in_dim(share_all, (my_index // 2) * block_rows, block_rows, 1)
    window = jnp.concatenate([window] * 3, axis=1)[:, :, None]
    if dense and clusters == blocks:
        outs = [out.reshape(1, hid_dev, half_cols) for out in deliver(owner[cluster_of], window, got)]
    else:
        merged = merge_blocks(owner[cluster_of], window, got, clusters)
        groups = [list(range(h, expert_count, 2)) for h in range(2)]
        final = lax.all_to_all(
            merged, "expert", split_axis=0, concat_axis=0, tiled=True, axis_index_groups=groups
        ).reshape(blocks, 3, block_rows, half_cols)
        outs = [final[:, i].reshape(1, hid_dev, half_cols) for i in range(3)]
    return (*outs, share)


def solution(mesh):
    return jax.shard_map(
        per_device,
        mesh=mesh,
        in_specs=(
            P(("expert", "dp"), None),
            P(("expert", "dp"), None),
            P(("expert", "dp"), None),
            P(("expert", "dp"), None),
            P("expert", "dp", None),
            P("expert", "dp", None),
            P("expert", "dp", None),
            P(),
            P(),
        ),
        out_specs=(
            P("expert", "dp", None),
            P("expert", "dp", None),
            P("expert", "dp", None),
            P("expert", "dp"),
        ),
        check_vma=False,
    )
```

profile of v0, /device:TPU:12, one launch (start us, length us, event | category | flops | bytes accessed | tf_op | source)
XLA Modules:
  0.0 209.6 jit_solution(16580827720105515295)
XLA Ops:
  0.6 0.0 copy-start
  0.6 0.0 copy-start.2
  0.7 1.3 multiply_reduce_fusion
  2.0 0.7 compare_select_fusion
  2.6 0.0 copy-done
  2.6 0.7 gather_fusion
  3.3 0.7 fusion.5
  4.0 0.1 copy.19
  4.1 0.8 copy.18
  4.9 0.4 select_reduce_fusion
  5.2 0.0 copy-done.2
  5.3 0.9 pad_maximum_fusion.tokens_ref
  6.1 0.0 copy-start.3
  6.1 139.6 %spread.1 = (bf16[16,3,48,1024]{3,2,1,0:T(8,128)(2,1)}, f32[16,1,384]{2,1,0:T(1,128)}) custom-call(bf16[128,2176]{1,0:T(8,128)(2,1)} %pad_maximum_fusion.tokens_ref, bf16[384,2048]{1,0:T(8,128)(2,1)} %bitcast.16, bf16[384,2048]{1,0:T(8,128)(2,1)} %bitcast.17, bf16[384,2048]{1,0:T(8,128)(2,1)} %bitcast.18), custom_call_target="tpu_custom_call" | custom-call | tf_op jit(solution)/shard_map/spread/pallas_call | solution.py:236
  145.7 0.0 copy-done.3
  145.7 0.9 convolution_divide_fusion
  146.7 0.6 constant_dynamic-slice_fusion
  147.3 0.1 constant_dynamic-slice_fusion.1
  147.3 0.1 maximum_bitcast_fusion
  147.4 0.5 copy.20.share_ref
  147.9 0.0 copy-start.1
  147.9 2.3 %copy-done.1 = bf16[16,3,48,1024]{3,2,1,0:T(8,128)(2,1)S(1)} copy-done((bf16[16,3,48,1024]{3,2,1,0:T(8,128)(2,1)S(1)}, bf16[16,3,48,1024]{3,2,1,0:T(8,128)(2,1)}, u32[]{:S(2)}) %copy-start.1) | copy-done | bytes 4718616
  150.2 56.7 %deliver.1 = (bf16[8,48,1024]{2,1,0:T(8,128)(2,1)S(1)}, bf16[8,48,1024]{2,1,0:T(8,128)(2,1)S(1)}, bf16[8,48,1024]{2,1,0:T(8,128)(2,1)S(1)}) custom-call(s32[16]{0:T(128)S(1)} %gather_fusion, f32[16,144,1]{2,1,0:T(8,128)S(1)} %copy.20.share_ref, bf16[16,144,1024]{2,1,0:T(8,128)(2,1)S(1)} %bitcast.12), custom_call_target="tpu_custom_call" | custom-call | tf_op jit(solution)/shard_map/deliver/pallas_call | solution.py:418
  206.9 0.9 copy.29
  207.8 0.9 copy.30
  208.7 0.9 copy.31
  (2 shorter events, 0.0 us)
Async XLA Ops:
  0.6 2.0 copy-start
  0.6 4.6 %copy-start.2 = (bf16[128,2048]{1,0:T(8,128)(2,1)S(1)}, bf16[128,2048]{1,0:T(8,128)(2,1)}, u32[]{:S(2)}) copy-start(bf16[128,2048]{1,0:T(8,128)(2,1)} %param.9) | copy-start | bytes 1572868
  6.1 139.6 %copy-start.3 = (s32[16]{0:T(128)S(1)}, s32[16]{0:T(128)}, u32[]{:S(2)}) copy-start(s32[16]{0:T(128)} %param.16) | copy-start | bytes 196
  147.9 2.3 %copy-start.1 = (bf16[16,3,48,1024]{3,2,1,0:T(8,128)(2,1)S(1)}, bf16[16,3,48,1024]{3,2,1,0:T(8,128)(2,1)}, u32[]{:S(2)}) copy-start(bf16[16,3,48,1024]{3,2,1,0:T(8,128)(2,1)} %get-tuple-element.10) | copy-start | bytes 14155780
where the time goes:
time: 210 us
  Pallas kernels  196 us (93%)
  local copies, waits for them, and re-layouts  7.65 us (4%)
  other arithmetic  3.95 us (2%)
    pallas_call x1, Pallas kernels, spread(): pl.pallas_call(functools.partial(spread_kernel, factor=1.0 / float(model_...  140 us
    pallas_call x1, Pallas kernels, deliver(): pl.pallas_call(deliver_kernel, out_shape=tuple((jax.ShapeDtypeStruct((chi...  56.7 us
    unnamed x12, local copies, waits for them, and re-layouts  5.78 us

commit v1 on v0

--- a/solution.py
+++ b/solution.py
@@ -66,7 +66,7 @@
     across = z * 4 + (1 - y) * 2 + core
     partner = z * 4 + y * 2 + (1 - core)
 
-    def line(act):
+    def own_line(act):
         source = tokens_ref
         for sign, kind in ((1, 0), (-1, 1)):
             @pl.when((z + sign >= 0) & (z + sign < depth))
@@ -74,6 +74,8 @@
                 act(token_copy(me, kind, me + 4 * sign, source), None)
         act(token_copy(me, 2, across, source), None)
         act(token_copy(me, 3, partner, source), None)
+
+    def line(act):
         for distance in range(1, depth):
             for sign, kind in ((1, 0), (-1, 1)):
                 origin = z - sign * distance
@@ -135,9 +137,12 @@
     swaps = [swap_copy(shift, which) for shift in range(1, dp_count) for which in range(2)]
     for copy in swaps:
         copy.start()
+    own_line(begin)
+    for peer in peers:
+        piece_copy(0, peer, me).start()
     line(begin)
     for peer in peers:
-        for which in range(3):
+        for which in range(1, 3):
             piece_copy(which, peer, me).start()
     for copy in own:
         copy.wait()
@@ -209,6 +214,7 @@
 
     for peer in peers:
         share_copy(peer, me).start()
+    own_line(finish)
     line(finish)
     beside(finish)
     for copy in swaps:

time: 210 us -> 217 us (1.033)
  Pallas kernels: 196 us -> 204 us
    pallas_call x1, Pallas kernels: 140 us -> 147 us  [spread(): pl.pallas_call(functools.partial(spread_kernel, factor=1.0 / float(model_...]
where the time goes in v1:
time: 217 us
  Pallas kernels  204 us (94%)
  local copies, waits for them, and re-layouts  7.65 us (4%)
  other arithmetic  3.95 us (2%)
    pallas_call x1, Pallas kernels, spread(): pl.pallas_call(functools.partial(spread_kernel, factor=1.0 / float(model_...  147 us
    pallas_call x1, Pallas kernels, deliver(): pl.pallas_call(deliver_kernel, out_shape=tuple((jax.ShapeDtypeStruct((chi...  56.7 us
    unnamed x12, local copies, waits for them, and re-layouts  5.78 us

profile of v1, /device:TPU:12, one launch (start us, length us, event | category | flops | bytes accessed | tf_op | source)
XLA Modules:
  0.0 216.9 jit_solution(6774960523266984328)
XLA Ops:
  0.6 0.0 copy-start
  0.6 0.0 copy-start.2
  0.7 1.3 multiply_reduce_fusion
  2.0 0.7 compare_select_fusion
  2.6 0.0 copy-done
  2.6 0.7 gather_fusion
  3.3 0.7 fusion.5
  4.0 0.1 copy.19
  4.1 0.8 copy.18
  4.9 0.4 select_reduce_fusion
  5.2 0.0 copy-done.2
  5.3 0.9 pad_maximum_fusion.tokens_ref
  6.1 0.0 copy-start.3
  6.1 146.9 %spread.1 = (bf16[16,3,48,1024]{3,2,1,0:T(8,128)(2,1)}, f32[16,1,384]{2,1,0:T(1,128)}) custom-call(bf16[128,2176]{1,0:T(8,128)(2,1)} %pad_maximum_fusion.tokens_ref, bf16[384,2048]{1,0:T(8,128)(2,1)} %bitcast.16, bf16[384,2048]{1,0:T(8,128)(2,1)} %bitcast.17, bf16[384,2048]{1,0:T(8,128)(2,1)} %bitcast.18), custom_call_target="tpu_custom_call" | custom-call | tf_op jit(solution)/shard_map/spread/pallas_call | solution.py:242
  153.0 0.0 copy-done.3
  153.0 0.9 convolution_divide_fusion
  154.0 0.6 constant_dynamic-slice_fusion
  154.5 0.1 constant_dynamic-slice_fusion.1
  154.6 0.1 maximum_bitcast_fusion
  154.7 0.5 copy.20.share_ref
  155.2 0.0 copy-start.1
  155.2 2.3 %copy-done.1 = bf16[16,3,48,1024]{3,2,1,0:T(8,128)(2,1)S(1)} copy-done((bf16[16,3,48,1024]{3,2,1,0:T(8,128)(2,1)S(1)}, bf16[16,3,48,1024]{3,2,1,0:T(8,128)(2,1)}, u32[]{:S(2)}) %copy-start.1) | copy-done | bytes 4718616
  157.5 56.7 %deliver.1 = (bf16[8,48,1024]{2,1,0:T(8,128)(2,1)S(1)}, bf16[8,48,1024]{2,1,0:T(8,128)(2,1)S(1)}, bf16[8,48,1024]{2,1,0:T(8,128)(2,1)S(1)}) custom-call(s32[16]{0:T(128)S(1)} %gather_fusion, f32[16,144,1]{2,1,0:T(8,128)S(1)} %copy.20.share_ref, bf16[16,144,1024]{2,1,0:T(8,128)(2,1)S(1)} %bitcast.12), custom_call_target="tpu_custom_call" | custom-call | tf_op jit(solution)/shard_map/deliver/pallas_call | solution.py:424
  214.2 0.9 copy.29
  215.1 0.9 copy.30
  216.0 0.9 copy.31
  (2 shorter events, 0.0 us)
Async XLA Ops:
  0.6 2.0 copy-start
  0.6 4.6 %copy-start.2 = (bf16[128,2048]{1,0:T(8,128)(2,1)S(1)}, bf16[128,2048]{1,0:T(8,128)(2,1)}, u32[]{:S(2)}) copy-start(bf16[128,2048]{1,0:T(8,128)(2,1)} %param.9) | copy-start | bytes 1572868
  6.1 146.9 %copy-start.3 = (s32[16]{0:T(128)S(1)}, s32[16]{0:T(128)}, u32[]{:S(2)}) copy-start(s32[16]{0:T(128)} %param.16) | copy-start | bytes 196
  155.2 2.3 %copy-start.1 = (bf16[16,3,48,1024]{3,2,1,0:T(8,128)(2,1)S(1)}, bf16[16,3,48,1024]{3,2,1,0:T(8,128)(2,1)}, u32[]{:S(2)}) copy-start(bf16[16,3,48,1024]{3,2,1,0:T(8,128)(2,1)} %get-tuple-element.10) | copy-start | bytes 14155780

commit v2 on v1

v2 whole, which is shorter than its diff:
```python
import functools

import jax
import jax.numpy as jnp
from jax import lax
from jax.experimental import pallas as pl
from jax.experimental.pallas import tpu as pltpu
from jax.sharding import PartitionSpec as P

LANES = 128
MESH = pl.DeviceIdType.MESH


def fused_kernel(
    cluster_ref, owner_ref, routes_ref, route_weight_ref, tokens_ref, cotangent_ref, gate_ref, up_ref, down_ref,
    out_gate_ref, out_up_ref, out_down_ref, share_ref,
    rows_ref, slope_ref, held_ref, parts_ref, others_ref, fisher_ref, all_ref, turned_ref, coef_ref, got_ref,
    merged_ref,
    token_send, token_recv, swap_send, swap_recv, part_send, part_recv, fisher_send, fisher_recv,
    piece_send, piece_recv, out_send, out_recv, own_sem, keep_sem,
    *, factor,
):
    experts, dp_count = lax.axis_size("expert"), lax.axis_size("dp")
    depth, chips = experts // 4, experts // 2
    me, my_dp = lax.axis_index("expert"), lax.axis_index("dp")
    z, y, core = me // 4, (me // 2) % 2, me % 2
    chip = me // 2
    row_count = tokens_ref.shape[0]
    hid_dev, model_width = gate_ref.shape
    half_cols = model_width // 2
    piece_rows = got_ref.shape[2]
    weights = (gate_ref, up_ref, down_ref)
    outs = (out_gate_ref, out_up_ref, out_down_ref)
    half_depth = depth // 2
    far_z, near_z = (1 - z // half_depth) * half_depth, z // half_depth * half_depth
    far_peers = [
        (far_z + (z + dz) % half_depth) * 4 + (me + k) % 4 for k in (0, 2, 1, 3) for dz in range(half_depth)
    ]
    near_peers = [
        (near_z + (z + dz) % half_depth) * 4 + (me + k) % 4 for dz in range(1, half_depth) for k in (0, 2, 1, 3)
    ] + [z * 4 + (me + k) % 4 for k in (2, 1, 3)]
    peers = far_peers + near_peers
    dp_of = [(my_dp + k) % dp_count for k in range(dp_count)]
    across = z * 4 + (1 - y) * 2 + core
    partner = z * 4 + y * 2 + (1 - core)

    def block_of(which, target):
        return weights[which].at[
            pl.ds((target // 2) * piece_rows, piece_rows), pl.ds((target % 2) * half_cols, half_cols)
        ]

    barrier = pltpu.get_barrier_semaphore()
    for peer in peers:
        pl.semaphore_signal(barrier, inc=1, device_id={"expert": peer}, device_id_type=MESH)
    for other in dp_of[1:]:
        pl.semaphore_signal(barrier, inc=1, device_id={"dp": other}, device_id_type=MESH)
    own = [
        pltpu.make_async_copy(gate_ref, held_ref.at[0, 0], own_sem.at[1]),
        pltpu.make_async_copy(up_ref, held_ref.at[0, 1], own_sem.at[2]),
    ] + [
        pltpu.make_async_copy(block_of(which, me), got_ref.at[me, which], own_sem.at[3 + which])
        for which in range(3)
    ]
    first = [
        pltpu.make_async_copy(cotangent_ref, slope_ref, own_sem.at[6]),
        pltpu.make_async_copy(tokens_ref, rows_ref.at[me, :, pl.ds(0, model_width)], own_sem.at[0]),
    ]
    for copy in first + own:
        copy.start()
    first[0].wait()
    slope = slope_ref[...].astype(jnp.float32)
    energy = jnp.sum(slope * slope, axis=1, keepdims=True) / float(model_width)
    energy_row = jnp.transpose(jnp.broadcast_to(energy, (row_count, LANES)))[:routes_ref.shape[0]]
    scale_row = jnp.square(route_weight_ref[...]) * energy_row
    expert_at = lax.broadcasted_iota(jnp.int32, (LANES, row_count), 0)
    scale_of = jnp.zeros((LANES, row_count), jnp.float32)
    for choice in range(routes_ref.shape[0]):
        chosen = routes_ref[choice:choice + 1] == expert_at
        scale_of = scale_of + jnp.where(chosen, scale_row[choice:choice + 1], 0.0)
    rows_ref[me, :, model_width:] = jnp.transpose(scale_of).astype(jnp.bfloat16)
    first[1].wait()
    pl.semaphore_wait(barrier, experts - 1 + dp_count - 1)

    def token_copy(slot, kind, peer, source=None):
        return pltpu.make_async_remote_copy(
            src_ref=rows_ref.at[slot] if source is None else source,
            dst_ref=rows_ref.at[slot],
            send_sem=token_send.at[kind, slot],
            recv_sem=token_recv.at[slot],
            device_id={"expert": peer},
            device_id_type=MESH,
        )

    def own_line(act):
        for sign, kind in ((1, 0), (-1, 1)):
            @pl.when((z + sign >= 0) & (z + sign < depth))
            def _():
                act(token_copy(me, kind, me + 4 * sign), None)
        act(token_copy(me, 2, across), None)
        act(token_copy(me, 3, partner), None)

    def line(act, distance):
        for sign, kind in ((1, 0), (-1, 1)):
            origin = z - sign * distance

            @pl.when((origin >= 0) & (origin < depth))
            def _():
                slot = origin * 4 + y * 2 + core
                act(None, slot)

                @pl.when((z + sign >= 0) & (z + sign < depth))
                def _():
                    act(token_copy(slot, kind, me + 4 * sign), None)
                act(token_copy(slot, 2, across), None)
                act(token_copy(slot, 3, partner), None)

    def beside(act):
        for distance in range(depth):
            for sign in (1, -1) if distance else (1,):
                origin = z - sign * distance

                @pl.when((origin >= 0) & (origin < depth))
                def _():
                    slot = origin * 4 + (1 - y) * 2 + core
                    act(None, slot)
                    act(token_copy(slot, 3, partner), None)

    def begin(copy, slot):
        if copy is None:
            token_copy(slot, 0, partner).wait_recv()
        else:
            copy.start()

    def finish(copy, slot):
        if copy is not None:
            copy.wait_send()

    def swap_copy(shift, which):
        return pltpu.make_async_remote_copy(
            src_ref=weights[which],
            dst_ref=held_ref.at[shift, which],
            send_sem=swap_send.at[shift, which],
            recv_sem=swap_recv.at[shift, which],
            device_id={"dp": dp_of[(dp_count - shift) % dp_count]},
            device_id_type=MESH,
        )

    def piece_copy(which, peer, landing):
        return pltpu.make_async_remote_copy(
            src_ref=block_of(which, peer),
            dst_ref=got_ref.at[landing, which],
            send_sem=piece_send.at[peer, which],
            recv_sem=piece_recv.at[landing, which],
            device_id={"expert": peer},
            device_id_type=MESH,
        )

    def pieces(which, targets):
        for peer in targets:
            piece_copy(which, peer, me).start()

    swaps = [swap_copy(shift, which) for shift in range(1, dp_count) for which in range(2)]
    for copy in swaps:
        copy.start()
    own_line(begin)
    for distance in range(1, depth):
        line(begin, distance)
    pieces(0, far_peers)
    pieces(1, far_peers)
    pieces(2, far_peers)
    for copy in own:
        copy.wait()
    beside(begin)
    for zs in range(depth):
        for ys in range(2):
            token_copy(zs * 4 + ys * 2 + 1 - core, 0, partner).wait_recv()

    for which in range(3):
        pieces(which, near_peers)

    contract = (((1,), (1,)), ((), ()))
    group = 4

    def compute(shift):
        parts_ref[shift] = jnp.zeros_like(parts_ref[shift])

        def step(index, carry):
            block = rows_ref[pl.ds(index * group, group)].reshape(group * row_count, rows_ref.shape[2])
            tokens = block[:, :model_width]
            pre_gate = lax.dot_general(
                tokens, held_ref[shift, 0], contract, preferred_element_type=jnp.float32) * factor
            pre_up = lax.dot_general(
                tokens, held_ref[shift, 1], contract, preferred_element_type=jnp.float32) * factor
            act = pre_gate / (1.0 + jnp.exp(-pre_gate)) * pre_up
            columns = block[:, model_width:].astype(jnp.float32)
            lane = lax.broadcasted_iota(jnp.int32, columns.shape, 1)
            scale = jnp.sum(jnp.where(lane == me, columns, 0.0), axis=1, keepdims=True)
            parts_ref[shift] += jnp.sum(act * act * scale, axis=0, keepdims=True)
            return carry

        lax.fori_loop(0, experts // group, step, 0)

    compute(0)
    for shift in range(1, dp_count):
        for which in range(2):
            swap_copy(shift, which).wait_recv()
        compute(shift)

    def part_copy(shift):
        return pltpu.make_async_remote_copy(
            src_ref=parts_ref.at[shift],
            dst_ref=others_ref.at[shift],
            send_sem=part_send.at[shift],
            recv_sem=part_recv.at[shift],
            device_id={"dp": dp_of[shift]},
            device_id_type=MESH,
        )

    for shift in range(1, dp_count):
        part_copy(shift).start()
    total = parts_ref[0]
    for shift in range(1, dp_count):
        part_copy(shift).wait()
        total = total + others_ref[shift]
    fisher_ref[me] = total

    def fisher_copy(peer, landing):
        return pltpu.make_async_remote_copy(
            src_ref=fisher_ref.at[me],
            dst_ref=fisher_ref.at[landing],
            send_sem=fisher_send.at[peer],
            recv_sem=fisher_recv.at[landing],
            device_id={"expert": peer},
            device_id_type=MESH,
        )

    for peer in peers:
        fisher_copy(peer, me).start()
    all_ref[...] = jnp.zeros_like(all_ref)
    for peer in peers:
        pltpu.make_async_remote_copy(
            src_ref=fisher_ref.at[me], dst_ref=fisher_ref.at[peer], send_sem=fisher_send.at[peer],
            recv_sem=fisher_recv.at[peer], device_id={"expert": peer}, device_id_type=MESH,
        ).wait_recv()

    def same_place(left, right):
        return jnp.where(cluster_ref[left] == cluster_ref[right], 1.0, 0.0)

    lane = lax.broadcasted_iota(jnp.int32, (1, LANES), 1)
    lane_place = jnp.full((1, LANES), -1, jnp.int32)
    for expert in range(experts):
        lane_place = jnp.where(lane == expert, owner_ref[cluster_ref[expert]], lane_place)

    for expert in range(experts):
        total = jnp.zeros((1, hid_dev), jnp.float32)
        for other in range(experts):
            total = total + fisher_ref[other] * same_place(expert, other)
        all_ref[expert:expert + 1] = fisher_ref[expert] / total
    share_ref[...] = all_ref[pl.ds(me, 1)]
    turned_ref[...] = jnp.transpose(all_ref[...])
    window = turned_ref[pl.ds(pl.multiple_of(chip * piece_rows, 16), piece_rows)]
    for place in range(chips):
        coef_ref[place] = jnp.where(lane_place == place, window, 0.0)

    def out_copy(which, place, landing):
        return pltpu.make_async_remote_copy(
            src_ref=merged_ref.at[which, place],
            dst_ref=outs[which].at[landing],
            send_sem=out_send.at[which, place],
            recv_sem=out_recv.at[which, landing],
            device_id={"expert": 2 * place + core},
            device_id_type=MESH,
        )

    tall, wide = 16, 512
    half_chips = chips // 2
    far_places = [far_z * 2 + (chip + k) % half_chips for k in range(half_chips)]
    near_places = [near_z * 2 + (chip + k) % half_chips for k in range(1, half_chips)] + [chip]

    def merge(which, places):
        def rows(index, carry):
            at = pl.ds(pl.multiple_of(index * tall, tall), tall)
            scales = [coef_ref[place, at] for place in places]
            for left in range(0, half_cols, wide):
                sums = [jnp.zeros((tall, wide), jnp.float32) for _ in places]
                for expert in range(experts):
                    block = got_ref[expert, which, at, left:left + wide].astype(jnp.float32)
                    sums = [
                        total + block * scale[:, expert:expert + 1] for total, scale in zip(sums, scales)
                    ]
                for place, total in zip(places, sums):
                    merged_ref[which, place, at, left:left + wide] = total.astype(jnp.bfloat16)
            return carry

        lax.fori_loop(0, piece_rows // tall, rows, 0)
        for place in places:
            if place is not chip:
                out_copy(which, place, chip).start()

    def arrived(which):
        for peer in peers:
            piece_copy(which, peer, peer).wait_recv()

    for which in range(2):
        arrived(which)
        merge(which, far_places)
    for which in range(2):
        merge(which, near_places)
    arrived(2)
    merge(2, far_places)
    merge(2, near_places)
    keep = [
        pltpu.make_async_copy(merged_ref.at[which, chip], outs[which].at[chip], keep_sem.at[which])
        for which in range(3)
    ]
    for copy in keep:
        copy.start()

    own_line(finish)
    for distance in range(1, depth):
        line(finish, distance)
    beside(finish)
    for copy in swaps:
        copy.wait_send()
    for peer in peers:
        fisher_copy(peer, me).wait_send()
        for which in range(3):
            piece_copy(which, peer, me).wait_send()
    for copy in keep:
        copy.wait()
    for which in range(3):
        for place in far_places + near_places[:-1]:
            out_copy(which, place, chip).wait_send()
            out_copy(which, place, place).wait_recv()


def fused(tokens, cotangent, routes, route_weight, gate, up, down, cluster_of, owner):
    experts, dp_count = lax.axis_size("expert"), lax.axis_size("dp")
    row_count, model_width = tokens.shape
    hid_dev, wide = gate.shape[0], model_width + LANES
    chips, half_cols = experts // 2, model_width // 2
    piece_rows = hid_dev // chips
    smem = pl.BlockSpec(memory_space=pltpu.SMEM)
    anywhere = pl.BlockSpec(memory_space=pl.ANY)
    vmem = pl.BlockSpec(memory_space=pltpu.VMEM)
    dma = pltpu.SemaphoreType.DMA
    narrow, full = jnp.bfloat16, jnp.float32
    *outs, share = pl.pallas_call(
        functools.partial(fused_kernel, factor=1.0 / float(model_width) ** 0.5),
        out_shape=tuple(jax.ShapeDtypeStruct((chips, piece_rows, half_cols), narrow) for _ in range(3)) + (
            jax.ShapeDtypeStruct((1, hid_dev), full),),
        in_specs=[smem, smem, vmem, vmem] + [anywhere] * 5,
        out_specs=(anywhere,) * 3 + (vmem,),
        scratch_shapes=[
            pltpu.VMEM((experts, row_count, wide), narrow),
            pltpu.VMEM((row_count, model_width), narrow),
            pltpu.VMEM((dp_count, 2, hid_dev, model_width), narrow),
            pltpu.VMEM((dp_count, 1, hid_dev), full),
            pltpu.VMEM((dp_count, 1, hid_dev), full),
            pltpu.VMEM((experts, 1, hid_dev), full),
            pltpu.VMEM((LANES, hid_dev), full),
            pltpu.VMEM((hid_dev, LANES), full),
            pltpu.VMEM((chips, piece_rows, LANES), full),
            pltpu.VMEM((experts, 3, piece_rows, half_cols), narrow),
            pltpu.VMEM((3, chips, piece_rows, half_cols), narrow),
            dma((4, experts)), dma((experts,)),
            dma((dp_count, 2)), dma((dp_count, 2)),
            dma((dp_count,)), dma((dp_count,)),
            dma((experts,)), dma((experts,)),
            dma((experts, 3)), dma((experts, 3)),
            dma((3, chips)), dma((3, chips)),
            dma((7,)), dma((3,)),
        ],
        compiler_params=pltpu.CompilerParams(
            collective_id=0, has_side_effects=True, vmem_limit_bytes=60 * 1024 * 1024
        ),
        name="fused",
    )(cluster_of, owner, routes.T, route_weight.T, tokens, cotangent, gate, up, down)
    return tuple(out.reshape(1, hid_dev, half_cols) for out in outs) + (share,)


def merge_kernel(place_ref, share_ref, got_ref, out_ref, total_ref):
    total_ref[...] = jnp.zeros_like(total_ref)

    def add(expert, carry):
        place = place_ref[expert]
        weighted = got_ref[expert].astype(jnp.float32) * share_ref[expert]
        total_ref[place] = total_ref[place] + weighted
        return carry

    lax.fori_loop(0, got_ref.shape[0], add, 0)
    out_ref[...] = total_ref[...].astype(jnp.bfloat16)


def merge_blocks(place, share, got, clusters):
    shape = (clusters,) + got.shape[1:]
    return pl.pallas_call(
        merge_kernel,
        out_shape=jax.ShapeDtypeStruct(shape, jnp.bfloat16),
        in_specs=[
            pl.BlockSpec(memory_space=pltpu.SMEM),
            pl.BlockSpec(memory_space=pltpu.VMEM),
            pl.BlockSpec(memory_space=pltpu.VMEM),
        ],
        out_specs=pl.BlockSpec(memory_space=pltpu.VMEM),
        scratch_shapes=[pltpu.VMEM(shape, jnp.float32)],
        cost_estimate=pl.CostEstimate(flops=2 * got.size, bytes_accessed=3 * got.size, transcendentals=0),
        name="merge",
    )(place, share, got)


def routed_fisher(tokens, scales, routes, gate_weight, up_weight, capacity):
    expert_count = lax.axis_size("expert")
    row_count, model_width = tokens.shape
    top_count = routes.shape[1]
    scales = scales.reshape(-1)
    flat_ids = routes.reshape(-1)
    one_hot = (flat_ids[:, None] == jnp.arange(expert_count, dtype=jnp.int32)[None, :]).astype(
        jnp.int32
    )
    rank_ids = jnp.sum((jnp.cumsum(one_hot, axis=0) - one_hot) * one_hot, axis=1)
    slot_ids = flat_ids * capacity + rank_ids
    source = jnp.arange(row_count * top_count, dtype=jnp.int32) // top_count
    send_rows = (
        jnp.zeros((expert_count * capacity, model_width), jnp.bfloat16)
        .at[slot_ids]
        .set(tokens[source])
    )
    send_scales = jnp.zeros((expert_count * capacity,), jnp.bfloat16).at[slot_ids].set(scales)
    recv_rows, recv_scales = (
        lax.all_to_all(
            send_rows.reshape(expert_count, capacity, model_width),
            "expert",
            split_axis=0,
            concat_axis=0,
            tiled=True,
        ),
        lax.all_to_all(
            send_scales.reshape(expert_count, capacity),
            "expert",
            split_axis=0,
            concat_axis=0,
            tiled=True,
        ),
    )
    inputs = recv_rows.reshape(-1, model_width)
    weights_s = recv_scales.reshape(-1).astype(jnp.float32)
    hid_dev = gate_weight.shape[1]
    factor = 1.0 / jnp.sqrt(jnp.float32(model_width))
    pre_gate = (
        jnp.dot(
            inputs,
            lax.all_gather(gate_weight[0], "dp", axis=0, tiled=True).T,
            preferred_element_type=jnp.float32,
        )
        * factor
    )
    pre_up = (
        jnp.dot(
            inputs,
            lax.all_gather(up_weight[0], "dp", axis=0, tiled=True).T,
            preferred_element_type=jnp.float32,
        )
        * factor
    )
    act = jax.nn.silu(pre_gate) * pre_up
    part = jnp.dot(weights_s, act * act, precision=lax.Precision.HIGHEST)
    whole_sum = lax.psum(part, "dp")
    own_fisher = lax.dynamic_slice_in_dim(whole_sum, lax.axis_index("dp") * hid_dev, hid_dev)
    return lax.all_gather(own_fisher[None, :], "expert", axis=0, tiled=True)


def exchange(*weights):
    expert_count = lax.axis_size("expert")
    blocks, (_, hid_dev, model_width) = expert_count // 2, weights[0].shape

    def split(weight):
        return weight[0].reshape(blocks, hid_dev // blocks, 2, model_width // 2).transpose(0, 2, 1, 3)

    sent = jnp.stack([split(w) for w in weights], axis=2)
    sent = sent.reshape(expert_count, 3 * (hid_dev // blocks), model_width // 2)
    return lax.all_to_all(sent, "expert", split_axis=0, concat_axis=0, tiled=True)


def per_device(
    tokens, cotangent, routes, route_weight, gate_weight, up_weight, down_weight, cluster_of, owner
):
    expert_count = lax.axis_size("expert")
    row_count, model_width = tokens.shape
    top_count = routes.shape[1]
    capacity = max(2, row_count * top_count * 9 // (8 * expert_count))
    hid_dev = gate_weight.shape[1]
    half_cols = model_width // 2
    blocks = expert_count // 2
    block_rows = hid_dev // blocks

    dense = row_count <= 2 * capacity and expert_count % 8 == 0 and block_rows % 16 == 0
    tiled = row_count % LANES == 0 and expert_count <= LANES
    clusters = owner.shape[0]
    if dense and tiled and clusters == blocks:
        return fused(
            tokens, cotangent, routes, route_weight, gate_weight[0], up_weight[0], down_weight[0], cluster_of, owner)
    place = owner[cluster_of]
    energy = jnp.mean(jnp.square(cotangent.astype(jnp.float32)), axis=1)
    scales = (jnp.square(route_weight) * energy[:, None]).astype(jnp.bfloat16)
    got = exchange(gate_weight, up_weight, down_weight)
    peer_fisher = routed_fisher(tokens, scales, routes, gate_weight, up_weight, capacity)
    same = (cluster_of[None, :] == cluster_of[:, None]).astype(jnp.float32)
    share_all = peer_fisher / jnp.dot(same, peer_fisher, precision=lax.Precision.HIGHEST)
    my_index = lax.axis_index("expert")
    share = lax.dynamic_slice_in_dim(share_all, my_index, 1, 0)
    window = lax.dynamic_slice_in_dim(share_all, (my_index // 2) * block_rows, block_rows, 1)
    window = jnp.concatenate([window] * 3, axis=1)[:, :, None]
    merged = merge_blocks(place, window, got, clusters)
    groups = [list(range(h, expert_count, 2)) for h in range(2)]
    final = lax.all_to_all(
        merged, "expert", split_axis=0, concat_axis=0, tiled=True, axis_index_groups=groups
    ).reshape(blocks, 3, block_rows, half_cols)
    outs = [final[:, i].reshape(1, hid_dev, half_cols) for i in range(3)]
    return (*outs, share)


def solution(mesh):
    return jax.shard_map(
        per_device,
        mesh=mesh,
        in_specs=(
            P(("expert", "dp"), None),
            P(("expert", "dp"), None),
            P(("expert", "dp"), None),
            P(("expert", "dp"), None),
            P("expert", "dp", None),
            P("expert", "dp", None),
            P("expert", "dp", None),
            P(),
            P(),
        ),
        out_specs=(
            P("expert", "dp", None),
            P("expert", "dp", None),
            P("expert", "dp", None),
            P("expert", "dp"),
        ),
        check_vma=False,
    )
```

time: 217 us -> 203 us (0.935)
  the two profiles are of different devices: /device:TPU:12 before, /device:TPU:0 now
where the time goes in v2:
time: 203 us
  Pallas kernels  197 us (97%)
  local copies, waits for them, and re-layouts  4.51 us (2%)
    pallas_call x1, Pallas kernels, fused(): pl.pallas_call(functools.partial(fused_kernel, factor=1.0 / float(model_w...  197 us
    unnamed x10, local copies, waits for them, and re-layouts  4.51 us

profile of v2, /device:TPU:0, one launch (start us, length us, event | category | flops | bytes accessed | tf_op | source)
XLA Modules:
  0.0 202.6 jit_solution(5541989587124758276)
XLA Ops:
  0.6 197.4 %fused.1 = (bf16[8,48,1024]{2,1,0:T(8,128)(2,1)}, bf16[8,48,1024]{2,1,0:T(8,128)(2,1)}, bf16[8,48,1024]{2,1,0:T(8,128)(2,1)}, f32[1,384]{1,0:T(1,128)}) custom-call(s32[16]{0:T(128)} %cluster_ref.1, s32[8]{0:T(128)} %owner_ref.1, s32[8,128]{1,0:T(8,128)} %bitcast.14, f32[8,128]{1,0:T(8,128)} %bitcast.15, bf16[128,2048]{1,0:T(8,128)(2,1)} %tokens_ref.1, ...), custom_call_target="tpu_custom_call" | custom-call | tf_op jit(solution)/shard_map/fused/pallas_call | solution.py:348
  198.1 0.0 copy-start.1
  198.1 0.0 copy-start
  198.1 2.2 %copy.17 = bf16[1,384,1024]{2,1,0:T(8,128)(2,1)} copy(bf16[1,384,1024]{2,1,0:T(8,128)(2,1)} %bitcast.13) | data formatting | bytes 1572864
  200.3 0.0 copy-done.1
  200.3 0.0 copy-start.2
  200.3 0.9 copy.18
  201.1 0.0 copy-done
  201.1 0.9 copy.19
  202.0 0.0 copy-done.2
  202.0 0.6 copy.20
Async XLA Ops:
  198.1 2.2 %copy-start.1 = (bf16[8,48,1024]{2,1,0:T(8,128)(2,1)S(1)}, bf16[8,48,1024]{2,1,0:T(8,128)(2,1)}, u32[]{:S(2)}) copy-start(bf16[8,48,1024]{2,1,0:T(8,128)(2,1)} %get-tuple-element.9) | copy-start | bytes 2359300
  198.1 3.1 %copy-start = (bf16[8,48,1024]{2,1,0:T(8,128)(2,1)S(1)}, bf16[8,48,1024]{2,1,0:T(8,128)(2,1)}, u32[]{:S(2)}) copy-start(bf16[8,48,1024]{2,1,0:T(8,128)(2,1)} %get-tuple-element.10) | copy-start | bytes 2359300
  200.3 1.8 copy-start.2
